TPU v7x, 32 devices: a whole 2x2x4 slice. The times are simulated.
32 devices in a mesh: seq: 16 (over z, x, core), res: 2 (over y).
Axes of the slice: x: 2, y: 2, z: 4, core: 2. Of those that a mesh axis runs over, the one named last changes fastest.
Arguments:
- embedded_aligned_rows: bfloat16 [48, 256, 768], P('seq', 'res'), may hold values from -12 to 12
- norm_multiplier: float32 [768], replicated, may hold values from 0.1 to 1.9
- asker_projector: bfloat16 [768, 768], replicated, may hold values from -1 to 1
- matcher_projector: bfloat16 [768, 768], replicated, may hold values from -1 to 1
- content_projector: bfloat16 [768, 768], replicated, may hold values from -0.21875 to 0.21875
- final_projector: bfloat16 [768, 768], replicated, may hold values from -0.21875 to 0.21875
Outputs:
- mixed: bfloat16 [48, 256, 768], P('seq', 'res')
All inputs are finite; a program needn't handle non-finite values.
Results may differ from a plain program's by a relative error of at most 0.01.
Values may be sent and summed in bfloat16 or wider, within the bound.
No kernel may reach another device: no remote copies, remote signals or barrier semaphores. Data moves between devices by JAX's collectives and lax.ppermute only.
A program may use at most 64 MiB of HBM per device.

v0:
```python
import jax
import jax.numpy as jnp
from jax import lax
from jax.sharding import PartitionSpec as P

HEADS = 12


def standardize_rows(embedded_aligned_rows, norm_multiplier):
    content_array = embedded_aligned_rows.astype(jnp.float32)
    center = content_array - jnp.mean(content_array, axis=-1, keepdims=True)
    spread = jnp.mean(center * center, axis=-1, keepdims=True)
    return (center / jnp.sqrt(spread + 1e-05) * norm_multiplier).astype(jnp.bfloat16)


def body(
    embedded_aligned_rows,
    norm_multiplier,
    asker_projector,
    matcher_projector,
    content_projector,
    final_projector,
):
    row_portion, column_portion, embedding_dimension = embedded_aligned_rows.shape
    heads = HEADS
    hsize = embedding_dimension // heads
    unrolled_array = standardize_rows(embedded_aligned_rows, norm_multiplier).reshape(
        row_portion * column_portion, embedding_dimension
    )
    query = jnp.dot(unrolled_array, asker_projector, preferred_element_type=jnp.float32).astype(
        jnp.bfloat16
    )
    query = query.reshape(row_portion, column_portion, heads, hsize)
    key_local = jnp.dot(
        unrolled_array, matcher_projector, preferred_element_type=jnp.float32
    ).astype(jnp.bfloat16)
    key_local = key_local.reshape(row_portion, column_portion, embedding_dimension)
    value_local = jnp.dot(
        unrolled_array, content_projector, preferred_element_type=jnp.float32
    ).astype(jnp.bfloat16)
    value_local = value_local.reshape(row_portion, column_portion, embedding_dimension)
    total_seqs = row_portion * lax.axis_size("seq")
    scale = 1.0 / (jnp.sqrt(jnp.float32(hsize)) * jnp.sqrt(jnp.float32(total_seqs)))
    key_all, value_all = (
        lax.all_gather(key_local, "res", axis=1, tiled=True),
        lax.all_gather(value_local, "res", axis=1, tiled=True),
    )
    keys = key_all.reshape(row_portion, key_all.shape[1], heads, hsize)
    logits = jnp.einsum("sihe,sjhe->hij", query, keys, preferred_element_type=jnp.float32)
    share = lax.psum_scatter(logits, "seq", scatter_dimension=1, tiled=True)
    share_probs = jax.nn.softmax(share * scale, axis=-1).astype(jnp.bfloat16)
    probs = lax.all_gather(share_probs, "seq", axis=1, tiled=True)
    content_array = value_all.reshape(row_portion, value_all.shape[1], heads, hsize)
    attended = jnp.einsum(
        "hij,sjhe->sihe", probs, content_array, preferred_element_type=jnp.float32
    )
    attended = attended.astype(jnp.bfloat16).reshape(
        row_portion * column_portion, embedding_dimension
    )
    mixed = jnp.dot(attended, final_projector, preferred_element_type=jnp.float32).astype(
        jnp.bfloat16
    )
    return mixed.reshape(row_portion, column_portion, embedding_dimension)


def solution(mesh):
    placed = (P("seq", "res", None), P(), P(), P(), P(), P())
    return jax.shard_map(
        body, mesh=mesh, in_specs=placed, out_specs=P("seq", "res", None), check_vma=False
    )
```

profile of v0, /device:TPU:0, one launch (start us, length us, event | category | flops | bytes accessed | tf_op | source)
XLA Modules:
  0.0 134.4 jit_solution(8885785728018542669)
XLA Ops:
  6.5 0.0 copy-start
  6.5 0.0 copy-start.1
  6.5 0.0 copy-start.2
  6.5 0.0 all-gather.5.cloned.1.call-start
  6.5 1.4 %convert_reduce_fusion = f32[3,128]{1,0:T(4,128)S(1)} fusion(bf16[3,128,768]{2,1,0:T(8,128)(2,1)} %param.6), kind=kLoop, calls=%fused_computation.4 | loop fusion | flops 589440 | bytes 591360 | tf_op jit(solution)/shard_map/reduce_sum | solution.py:11
  7.9 1.4 %fusion.5 = f32[3,128]{1,0:T(4,128)S(1)} fusion(bf16[3,128,768]{2,1,0:T(8,128)(2,1)} %param.6, f32[3,128]{1,0:T(4,128)S(1)} %broadcast_multiply_fusion), kind=kLoop, calls=%fused_computation.13 | loop fusion | flops 1179264 | bytes 592896 | tf_op jit(solution)/shard_map/reduce_sum | solution.py:12
  9.3 0.0 copy-done.1
  9.3 0.0 copy-done.2
  9.3 0.2 fusion.7
  9.6 0.0 copy-done
  9.6 0.6 convolution_convert_fusion.2
  10.2 0.0 copy-start.3
  10.2 1.1 copy.10
  11.3 0.0 all-gather.5.cloned.1.call-update
  11.3 0.0 reduce-scatter.2.cloned.1.call-start
  11.3 0.3 copy-done.3
  11.7 1.4 %convolution_convert_fusion.3 = bf16[384,768]{1,0:T(8,128)(2,1)} fusion(bf16[384,768]{1,0:T(8,128)(2,1)S(1)} %bitcast.33, bf16[768,768]{1,0:T(8,128)(2,1)S(1)} %copy-done.3), kind=kOutput, calls=%fused_computation.10 | convolution fusion | flops 453279744 | bytes 2359296 | tf_op jit(solution)/shard_map/dot_general | solution.py:30
  13.1 1.9 %reshape.49 = bf16[3,128,12,64]{3,2,1,0:T(8,128)(2,1)S(1)} reshape(bf16[384,768]{1,0:T(8,128)(2,1)} %convolution_convert_fusion.3) | data formatting | bytes 1179648 | tf_op jit(solution)/shard_map/reshape | solution.py:33
  15.1 21.8 %all-gather.5.cloned.1.call-done = bf16[3,256,768]{1,2,0:T(8,128)(2,1)} async-done(((bf16[3,128,768]{1,2,0:T(8,128)(2,1)}), bf16[3,256,768]{1,2,0:T(8,128)(2,1)}) %all-gather.5.cloned.1.call-update) | async-done | bytes 1179664 | tf_op jit(solution)/shard_map/all_gather | solution.py:45
  36.9 2.9 %convolution_bitcast_fusion = f32[12,128,256]{2,1,0:T(8,128)} fusion(bf16[3,128,12,64]{3,2,1,0:T(8,128)(2,1)S(1)} %reshape.49, bf16[3,256,12,64]{1,3,2,0:T(8,128)(2,1)} %bitcast.30), kind=kOutput, calls=%fused_computation.2 | convolution fusion | flops 150994944 | bytes 3342336 | tf_op jit(solution)/shard_map/sihe,sjhe->hij/dot_general | solution.py:49
  39.8 0.0 copy-start.4
  39.8 0.0 reduce-scatter.2.cloned.1.call-update
  39.8 0.0 all-gather.3.cloned.1.call-start
  39.9 1.2 copy-done.4
  41.1 0.6 convolution_convert_fusion.4
  41.7 1.1 copy.8
  42.8 0.0 all-gather.3.cloned.1.call-update
  42.8 57.4 %reduce-scatter.2.cloned.1.call-done = f32[12,8,256]{2,1,0:T(8,128)} async-done(((f32[12,128,256]{2,1,0:T(8,128)}), f32[12,8,256]{2,1,0:T(8,128)}) %reduce-scatter.2.cloned.1.call-update) | async-done | bytes 98320 | tf_op jit(solution)/shard_map/reduce_scatter | solution.py:50
  100.1 1.1 fusion.14
  101.2 21.5 %all_gather.11 = bf16[12,128,256]{2,1,0:T(8,128)(2,1)S(1)} all-gather(bf16[12,8,256]{2,1,0:T(8,128)(2,1)S(1)} %fusion.14), channel_id=1, replica_groups=mesh['seq'=16,'res'=2] {'seq'}, dimensions={1}, use_global_device_ids=true | all-gather | bytes 835584 | tf_op jit(solution)/shard_map/all_gather | solution.py:52
  122.7 0.7 all-gather.3.cloned.1.call-done
  123.4 1.7 %fusion.4 = bf16[3,128,12,64]{1,3,0,2:T(8,128)(2,1)S(1)} fusion(bf16[3,256,12,64]{1,3,2,0:T(8,128)(2,1)} %bitcast.37, bf16[12,128,256]{2,1,0:T(8,128)(2,1)S(1)} %all_gather.11), kind=kOutput, calls=%fused_computation.12 | convolution fusion | flops 151289856 | bytes 2555904 | tf_op jit(solution)/shard_map/hij,sjhe->sihe/dot_general | solution.py:54
  125.2 0.0 copy-start.5
  125.2 0.5 copy.14
  125.7 0.7 copy-done.5
  126.4 1.5 %convolution_convert_fusion = bf16[384,768]{1,0:T(8,128)(2,1)} fusion(bf16[768,768]{1,0:T(8,128)(2,1)S(1)} %copy-done.5, bf16[96,8,3,128]{3,2,1,0:T(4,128)(2,1)S(1)} %bitcast.31), kind=kOutput, calls=%fused_computation.7 | convolution fusion | flops 453279744 | bytes 2359296 | tf_op jit(solution)/shard_map/dot_general | solution.py:60
  (2 shorter events, 0.0 us)
Async XLA Ops:
  6.5 3.0 %copy-start = (bf16[768,768]{1,0:T(8,128)(2,1)S(1)}, bf16[768,768]{1,0:T(8,128)(2,1)}, u32[]{:S(2)}) copy-start(bf16[768,768]{1,0:T(8,128)(2,1)} %param.9) | copy-start | bytes 3538948
  6.5 2.8 %copy-start.1 = (bf16[3,128,768]{2,1,0:T(8,128)(2,1)S(1)}, bf16[3,128,768]{2,1,0:T(8,128)(2,1)}, u32[]{:S(2)}) copy-start(bf16[3,128,768]{2,1,0:T(8,128)(2,1)} %param.6) | copy-start | bytes 1769476
  6.5 2.8 %copy-start.2 = (f32[768]{0:T(1024)S(1)}, f32[768]{0:T(1024)}, u32[]{:S(2)}) copy-start(f32[768]{0:T(1024)} %param.7) | copy-start | bytes 9220
  6.5 30.4 %all-gather.5.cloned.1.call-start = ((), (), s32[]{:S(2)}) async-start(), calls=%async_computation.2 | async-start | bytes 1769472 | tf_op jit(solution)/shard_map/all_gather | solution.py:45
  10.2 1.5 %copy-start.3 = (bf16[768,768]{1,0:T(8,128)(2,1)S(1)}, bf16[768,768]{1,0:T(8,128)(2,1)}, u32[]{:S(2)}) copy-start(bf16[768,768]{1,0:T(8,128)(2,1)} %param.8) | copy-start | bytes 3538948
  11.3 88.8 %reduce-scatter.2.cloned.1.call-start = ((), (), s32[]{:S(2)}) async-start(), calls=%async_computation.3 | async-start | bytes 1671168 | tf_op jit(solution)/shard_map/reduce_scatter | solution.py:50
  39.8 1.3 copy-start.4
  39.8 83.6 %all-gather.3.cloned.1.call-start = ((), (), s32[]{:S(2)}) async-start(), calls=%async_computation.1 | async-start | bytes 1769472 | tf_op jit(solution)/shard_map/all_gather | solution.py:46
  125.2 1.3 copy-start.5
Sparse Core Ops, SparseCore 0:
  11.4 25.4 all-gather.4
  40.6 59.5 reduce-scatter.1
  101.7 21.6 all-gather.2
where the time goes:
time: 135 us; the launch traced here: 134 us
  waiting for transfers between devices  79.9 us (59%)
  blocking collectives  21.5 us (16%)
  between operations  13.2 us (10%)
  matrix products  8.81 us (7%)
  local copies, waits for them, and re-layouts  6.86 us (5%)
  other arithmetic  4.05 us (3%)
    reduce_scatter x1, waiting for transfers between devices, body(): share = lax.psum_scatter(logits, 'seq', scatter_dimension=1, tiled=True)  57.4 us
    all_gather x1, waiting for transfers between devices, body(): lax.all_gather(key_local, 'res', axis=1, tiled=True)  21.8 us
    all_gather x1, blocking collectives, body(): probs = lax.all_gather(share_probs, 'seq', axis=1, tiled=True)  21.5 us
    dot_general x1, matrix products, body(): jnp.einsum('sihe,sjhe->hij', query, keys, preferred_element_type=jnp.floa...  2.9 us
  transfers between devices with their start and end apart: 3, of which 3 were waited for; matrix products, arithmetic and copies ran while one was open for 5% of the time, Pallas kernels for 0%

commit v1 on v0

--- a/solution.py
+++ b/solution.py
@@ -49,7 +49,12 @@
     logits = jnp.einsum("sihe,sjhe->hij", query, keys, preferred_element_type=jnp.float32)
     share = lax.psum_scatter(logits, "seq", scatter_dimension=1, tiled=True)
     share_probs = jax.nn.softmax(share * scale, axis=-1).astype(jnp.bfloat16)
-    probs = lax.all_gather(share_probs, "seq", axis=1, tiled=True)
+    ring = [share_probs]
+    for hop in range(15):
+        ring.append(lax.ppermute(ring[-1], "seq", [(dev, (dev + 1) % 16) for dev in range(16)]))
+    probs = jnp.roll(
+        jnp.concatenate(ring[::-1], axis=1), (lax.axis_index("seq") + 1) * ring[0].shape[1], axis=1
+    )
     content_array = value_all.reshape(row_portion, value_all.shape[1], heads, hsize)
     attended = jnp.einsum(
         "hij,sjhe->sihe", probs, content_array, preferred_element_type=jnp.float32

time: 135 us -> 227 us (1.68)
  waiting for transfers between devices: 79.9 us -> 172 us
  blocking collectives: 21.5 us -> 0 us
  local copies, waits for them, and re-layouts: 6.86 us -> 23.5 us
  matrix products: 8.81 us -> 11.7 us
    ppermute x0 -> x15, waiting for transfers between devices: none -> 90.1 us  [body(): lax.ppermute(ring[-1], 'seq', [(dev, (dev + 1) % 16) for dev in range(16)])]
    all_gather x1 -> x0, blocking collectives: 21.5 us -> none  [body(): probs = lax.all_gather(share_probs, 'seq', axis=1, tiled=True)]
    unnamed x12 -> x36, local copies, waits for them, and re-layouts: 2.3 us -> 18.9 us
    reduce_scatter x1, waiting for transfers between devices: 57.4 us -> 60.3 us  [body(): share = lax.psum_scatter(logits, 'seq', scatter_dimension=1, tiled=True)]
  transfers between devices with their start and end apart: 3 -> 18, of which waited for: 3 -> 18; matrix products, arithmetic and copies ran while one was open for 5% -> 12% of each run, Pallas kernels for 0% -> 0%
where the time goes in v1:
time: 227 us
  waiting for transfers between devices  172 us (76%)
  local copies, waits for them, and re-layouts  23.5 us (10%)
  between operations  13.3 us (6%)
  matrix products  11.7 us (5%)
  other arithmetic  6.26 us (3%)
    ppermute x15, waiting for transfers between devices, body(): lax.ppermute(ring[-1], 'seq', [(dev, (dev + 1) % 16) for dev in range(16)])  90.1 us
    reduce_scatter x1, waiting for transfers between devices, body(): share = lax.psum_scatter(logits, 'seq', scatter_dimension=1, tiled=True)  60.3 us
    all_gather x1, waiting for transfers between devices, body(): lax.all_gather(key_local, 'res', axis=1, tiled=True)  20.9 us
    unnamed x36, local copies, waits for them, and re-layouts  18.9 us
  transfers between devices with their start and end apart: 18, of which 18 were waited for; matrix products, arithmetic and copies ran while one was open for 12% of the time, Pallas kernels for 0%

profile of v1, /device:TPU:0, one launch (start us, length us, event | category | flops | bytes accessed | tf_op | source)
XLA Modules:
  0.0 226.6 jit_solution(11769689773727919017)
XLA Ops:
  6.5 1.4 convert_reduce_fusion
  7.9 1.4 fusion.4
  9.3 0.9 fusion.6
  10.9 1.1 copy.10
  12.0 2.7 %convolution_convert_fusion.3 = bf16[384,768]{1,0:T(8,128)(2,1)} fusion(bf16[384,768]{1,0:T(8,128)(2,1)S(1)} %bitcast.33, bf16[768,768]{1,0:T(8,128)(2,1)} %param.8), kind=kOutput, calls=%fused_computation.9 | convolution fusion | flops 453279744 | bytes 2359296 | tf_op jit(solution)/shard_map/dot_general | solution.py:30
  14.7 1.9 reshape.49
  16.7 20.9 %all-gather.5.cloned.1.call-done = bf16[3,256,768]{1,2,0:T(8,128)(2,1)} async-done(((bf16[3,128,768]{1,2,0:T(8,128)(2,1)}), bf16[3,256,768]{1,2,0:T(8,128)(2,1)}) %all-gather.5.cloned.1.call-update) | async-done | bytes 1179664 | tf_op jit(solution)/shard_map/all_gather | solution.py:45
  37.6 2.9 %convolution_bitcast_fusion = f32[12,128,256]{2,1,0:T(8,128)} fusion(bf16[3,128,12,64]{3,2,1,0:T(8,128)(2,1)S(1)} %reshape.49, bf16[3,256,12,64]{1,3,2,0:T(8,128)(2,1)} %bitcast.30), kind=kOutput, calls=%fused_computation.1 | convolution fusion | flops 150994944 | bytes 3342336 | tf_op jit(solution)/shard_map/sihe,sjhe->hij/dot_general | solution.py:49
  40.5 60.3 %reduce-scatter.2.cloned.1.call-done = f32[12,8,256]{2,1,0:T(8,128)} async-done(((f32[12,128,256]{2,1,0:T(8,128)}), f32[12,8,256]{2,1,0:T(8,128)}) %reduce-scatter.2.cloned.1.call-update) | async-done | bytes 98320 | tf_op jit(solution)/shard_map/reduce_scatter | solution.py:50
  100.8 1.1 fusion.20
  102.0 6.2 %collective-permute-done = bf16[12,8,256]{2,1,0:T(8,128)(2,1)S(1)} collective-permute-done((bf16[12,8,256]{2,1,0:T(8,128)(2,1)S(1)}, bf16[12,8,256]{2,1,0:T(8,128)(2,1)S(1)}, u32[]{:S(2)}, u32[]{:S(2)}) %collective-permute-start) | collective-permute-done | bytes 49184 | tf_op jit(solution)/shard_map/ppermute | solution.py:54
  108.2 6.2 %collective-permute-done.1 = bf16[12,8,256]{2,1,0:T(8,128)(2,1)S(1)} collective-permute-done((bf16[12,8,256]{2,1,0:T(8,128)(2,1)S(1)}, bf16[12,8,256]{2,1,0:T(8,128)(2,1)S(1)}, u32[]{:S(2)}, u32[]{:S(2)}) %collective-permute-start.1) | collective-permute-done | bytes 49184 | tf_op jit(solution)/shard_map/ppermute | solution.py:54
  114.4 6.2 %collective-permute-done.2 = bf16[12,8,256]{2,1,0:T(8,128)(2,1)S(1)} collective-permute-done((bf16[12,8,256]{2,1,0:T(8,128)(2,1)S(1)}, bf16[12,8,256]{2,1,0:T(8,128)(2,1)S(1)}, u32[]{:S(2)}, u32[]{:S(2)}) %collective-permute-start.2) | collective-permute-done | bytes 49184 | tf_op jit(solution)/shard_map/ppermute | solution.py:54
  120.7 6.2 %collective-permute-done.3 = bf16[12,8,256]{2,1,0:T(8,128)(2,1)S(1)} collective-permute-done((bf16[12,8,256]{2,1,0:T(8,128)(2,1)S(1)}, bf16[12,8,256]{2,1,0:T(8,128)(2,1)S(1)}, u32[]{:S(2)}, u32[]{:S(2)}) %collective-permute-start.3) | collective-permute-done | bytes 49184 | tf_op jit(solution)/shard_map/ppermute | solution.py:54
  126.9 6.2 %collective-permute-done.4 = bf16[12,8,256]{2,1,0:T(8,128)(2,1)S(1)} collective-permute-done((bf16[12,8,256]{2,1,0:T(8,128)(2,1)S(1)}, bf16[12,8,256]{2,1,0:T(8,128)(2,1)S(1)}, u32[]{:S(2)}, u32[]{:S(2)}) %collective-permute-start.4) | collective-permute-done | bytes 49184 | tf_op jit(solution)/shard_map/ppermute | solution.py:54
  133.1 6.2 %collective-permute-done.5 = bf16[12,8,256]{2,1,0:T(8,128)(2,1)S(1)} collective-permute-done((bf16[12,8,256]{2,1,0:T(8,128)(2,1)S(1)}, bf16[12,8,256]{2,1,0:T(8,128)(2,1)S(1)}, u32[]{:S(2)}, u32[]{:S(2)}) %collective-permute-start.5) | collective-permute-done | bytes 49184 | tf_op jit(solution)/shard_map/ppermute | solution.py:54
  139.3 6.2 %collective-permute-done.6 = bf16[12,8,256]{2,1,0:T(8,128)(2,1)S(1)} collective-permute-done((bf16[12,8,256]{2,1,0:T(8,128)(2,1)S(1)}, bf16[12,8,256]{2,1,0:T(8,128)(2,1)S(1)}, u32[]{:S(2)}, u32[]{:S(2)}) %collective-permute-start.6) | collective-permute-done | bytes 49184 | tf_op jit(solution)/shard_map/ppermute | solution.py:54
  145.5 6.2 %collective-permute-done.7 = bf16[12,8,256]{2,1,0:T(8,128)(2,1)S(1)} collective-permute-done((bf16[12,8,256]{2,1,0:T(8,128)(2,1)S(1)}, bf16[12,8,256]{2,1,0:T(8,128)(2,1)S(1)}, u32[]{:S(2)}, u32[]{:S(2)}) %collective-permute-start.7) | collective-permute-done | bytes 49184 | tf_op jit(solution)/shard_map/ppermute | solution.py:54
  151.7 6.2 %collective-permute-done.8 = bf16[12,8,256]{2,1,0:T(8,128)(2,1)S(1)} collective-permute-done((bf16[12,8,256]{2,1,0:T(8,128)(2,1)S(1)}, bf16[12,8,256]{2,1,0:T(8,128)(2,1)S(1)}, u32[]{:S(2)}, u32[]{:S(2)}) %collective-permute-start.8) | collective-permute-done | bytes 49184 | tf_op jit(solution)/shard_map/ppermute | solution.py:54
  157.9 6.2 %collective-permute-done.9 = bf16[12,8,256]{2,1,0:T(8,128)(2,1)S(1)} collective-permute-done((bf16[12,8,256]{2,1,0:T(8,128)(2,1)S(1)}, bf16[12,8,256]{2,1,0:T(8,128)(2,1)S(1)}, u32[]{:S(2)}, u32[]{:S(2)}) %collective-permute-start.9) | collective-permute-done | bytes 49184 | tf_op jit(solution)/shard_map/ppermute | solution.py:54
  164.1 6.2 %collective-permute-done.10 = bf16[12,8,256]{2,1,0:T(8,128)(2,1)S(1)} collective-permute-done((bf16[12,8,256]{2,1,0:T(8,128)(2,1)S(1)}, bf16[12,8,256]{2,1,0:T(8,128)(2,1)S(1)}, u32[]{:S(2)}, u32[]{:S(2)}) %collective-permute-start.10) | collective-permute-done | bytes 49184 | tf_op jit(solution)/shard_map/ppermute | solution.py:54
  170.4 6.2 %collective-permute-done.11 = bf16[12,8,256]{2,1,0:T(8,128)(2,1)S(1)} collective-permute-done((bf16[12,8,256]{2,1,0:T(8,128)(2,1)S(1)}, bf16[12,8,256]{2,1,0:T(8,128)(2,1)S(1)}, u32[]{:S(2)}, u32[]{:S(2)}) %collective-permute-start.11) | collective-permute-done | bytes 49184 | tf_op jit(solution)/shard_map/ppermute | solution.py:54
  176.6 6.2 %collective-permute-done.12 = bf16[12,8,256]{2,1,0:T(8,128)(2,1)S(1)} collective-permute-done((bf16[12,8,256]{2,1,0:T(8,128)(2,1)S(1)}, bf16[12,8,256]{2,1,0:T(8,128)(2,1)S(1)}, u32[]{:S(2)}, u32[]{:S(2)}) %collective-permute-start.12) | collective-permute-done | bytes 49184 | tf_op jit(solution)/shard_map/ppermute | solution.py:54
  182.8 6.2 %collective-permute-done.13 = bf16[12,8,256]{2,1,0:T(8,128)(2,1)S(1)} collective-permute-done((bf16[12,8,256]{2,1,0:T(8,128)(2,1)S(1)}, bf16[12,8,256]{2,1,0:T(8,128)(2,1)S(1)}, u32[]{:S(2)}, u32[]{:S(2)}) %collective-permute-start.13) | collective-permute-done | bytes 49184 | tf_op jit(solution)/shard_map/ppermute | solution.py:54
  189.0 1.9 convolution_convert_fusion.4
  190.9 1.1 copy.8
  192.0 3.2 %collective-permute-done.14 = bf16[12,8,256]{2,1,0:T(8,128)(2,1)S(1)} collective-permute-done((bf16[12,8,256]{2,1,0:T(8,128)(2,1)S(1)}, bf16[12,8,256]{2,1,0:T(8,128)(2,1)S(1)}, u32[]{:S(2)}, u32[]{:S(2)}) %collective-permute-start.14) | collective-permute-done | bytes 49184 | tf_op jit(solution)/shard_map/ppermute | solution.py:54
  195.8 0.6 constant_dynamic-update-slice_fusion.30
  197.1 0.6 constant_dynamic-update-slice_fusion.28
  199.0 0.6 constant_dynamic-update-slice_fusion.25
  200.2 0.6 constant_dynamic-update-slice_fusion.23
  200.9 0.6 constant_dynamic-update-slice_fusion.22
  201.5 0.7 constant_dynamic-update-slice_fusion.21
  202.2 0.6 constant_dynamic-update-slice_fusion.20
  202.8 0.6 constant_dynamic-update-slice_fusion.19
  203.4 0.6 constant_dynamic-update-slice_fusion.18
  204.1 0.6 constant_dynamic-update-slice_fusion.17
  204.7 0.7 constant_dynamic-update-slice_fusion.16
  205.4 0.6 constant_dynamic-update-slice_fusion.15
  206.1 0.6 constant_dynamic-update-slice_fusion.14
  207.9 0.6 constant_dynamic-update-slice_fusion.11
  208.6 0.6 constant_dynamic-update-slice_fusion.10
  209.8 0.6 constant_dynamic-update-slice_fusion.8
  212.3 0.6 constant_dynamic-update-slice_fusion.4
  214.2 0.6 constant_dynamic-update-slice_fusion.1
  214.9 0.7 constant_dynamic-update-slice_fusion
  216.0 2.0 fusion.3
  218.6 1.5 convolution_convert_fusion
  (46 shorter events, 10.0 us)
Async XLA Ops:
  6.5 3.7 %copy-start = (bf16[768,768]{1,0:T(8,128)(2,1)S(1)}, bf16[768,768]{1,0:T(8,128)(2,1)}, u32[]{:S(2)}) copy-start(bf16[768,768]{1,0:T(8,128)(2,1)} %param.9) | copy-start | bytes 3538948
  6.5 2.7 %copy-start.1 = (bf16[3,128,768]{2,1,0:T(8,128)(2,1)S(1)}, bf16[3,128,768]{2,1,0:T(8,128)(2,1)}, u32[]{:S(2)}) copy-start(bf16[3,128,768]{2,1,0:T(8,128)(2,1)} %param.6) | copy-start | bytes 1769476
  6.5 31.0 %all-gather.5.cloned.1.call-start = ((), (), s32[]{:S(2)}) async-start(), calls=%async_computation.2 | async-start | bytes 1769472 | tf_op jit(solution)/shard_map/all_gather | solution.py:45
  12.0 88.8 %reduce-scatter.2.cloned.1.call-start = ((), (), s32[]{:S(2)}) async-start(), calls=%async_computation.3 | async-start | bytes 1671168 | tf_op jit(solution)/shard_map/reduce_scatter | solution.py:50
  40.5 175.5 %all-gather.3.cloned.1.call-start = ((), (), s32[]{:S(2)}) async-start(), calls=%async_computation.1 | async-start | bytes 1769472 | tf_op jit(solution)/shard_map/all_gather | solution.py:46
  102.0 6.3 %collective-permute-start = (bf16[12,8,256]{2,1,0:T(8,128)(2,1)S(1)}, bf16[12,8,256]{2,1,0:T(8,128)(2,1)S(1)}, u32[]{:S(2)}, u32[]{:S(2)}) collective-permute-start(bf16[12,8,256]{2,1,0:T(8,128)(2,1)S(1)} %divide_convert_fusion), channel_id=1, source_target_pairs={{0,2},{2,4},{4,6},{6,8},{8,10},{10,12},{12,14},{14,16},{16,18},{18... | collective-permute-start | bytes 147464 | tf_op jit(solution)/shard_map/ppermute | solution.py:54
  108.2 6.2 %collective-permute-start.1 = (bf16[12,8,256]{2,1,0:T(8,128)(2,1)S(1)}, bf16[12,8,256]{2,1,0:T(8,128)(2,1)S(1)}, u32[]{:S(2)}, u32[]{:S(2)}) collective-permute-start(bf16[12,8,256]{2,1,0:T(8,128)(2,1)S(1)} %collective-permute-done), channel_id=1, source_target_pairs={{0,2},{2,4},{4,6},{6,8},{8,10},{10,12},{12,14},{14,16},{16,18},{18... | collective-permute-start | bytes 147464 | tf_op jit(solution)/shard_map/ppermute | solution.py:54
  114.4 6.2 %collective-permute-start.2 = (bf16[12,8,256]{2,1,0:T(8,128)(2,1)S(1)}, bf16[12,8,256]{2,1,0:T(8,128)(2,1)S(1)}, u32[]{:S(2)}, u32[]{:S(2)}) collective-permute-start(bf16[12,8,256]{2,1,0:T(8,128)(2,1)S(1)} %collective-permute-done.1), channel_id=1, source_target_pairs={{0,2},{2,4},{4,6},{6,8},{8,10},{10,12},{12,14},{14,16},{16,18},{18... | collective-permute-start | bytes 147464 | tf_op jit(solution)/shard_map/ppermute | solution.py:54
  120.6 6.2 %collective-permute-start.3 = (bf16[12,8,256]{2,1,0:T(8,128)(2,1)S(1)}, bf16[12,8,256]{2,1,0:T(8,128)(2,1)S(1)}, u32[]{:S(2)}, u32[]{:S(2)}) collective-permute-start(bf16[12,8,256]{2,1,0:T(8,128)(2,1)S(1)} %collective-permute-done.2), channel_id=1, source_target_pairs={{0,2},{2,4},{4,6},{6,8},{8,10},{10,12},{12,14},{14,16},{16,18},{18... | collective-permute-start | bytes 147464 | tf_op jit(solution)/shard_map/ppermute | solution.py:54
  126.9 6.2 %collective-permute-start.4 = (bf16[12,8,256]{2,1,0:T(8,128)(2,1)S(1)}, bf16[12,8,256]{2,1,0:T(8,128)(2,1)S(1)}, u32[]{:S(2)}, u32[]{:S(2)}) collective-permute-start(bf16[12,8,256]{2,1,0:T(8,128)(2,1)S(1)} %collective-permute-done.3), channel_id=1, source_target_pairs={{0,2},{2,4},{4,6},{6,8},{8,10},{10,12},{12,14},{14,16},{16,18},{18... | collective-permute-start | bytes 147464 | tf_op jit(solution)/shard_map/ppermute | solution.py:54
  133.1 6.2 %collective-permute-start.5 = (bf16[12,8,256]{2,1,0:T(8,128)(2,1)S(1)}, bf16[12,8,256]{2,1,0:T(8,128)(2,1)S(1)}, u32[]{:S(2)}, u32[]{:S(2)}) collective-permute-start(bf16[12,8,256]{2,1,0:T(8,128)(2,1)S(1)} %collective-permute-done.4), channel_id=1, source_target_pairs={{0,2},{2,4},{4,6},{6,8},{8,10},{10,12},{12,14},{14,16},{16,18},{18... | collective-permute-start | bytes 147464 | tf_op jit(solution)/shard_map/ppermute | solution.py:54
  139.3 6.2 %collective-permute-start.6 = (bf16[12,8,256]{2,1,0:T(8,128)(2,1)S(1)}, bf16[12,8,256]{2,1,0:T(8,128)(2,1)S(1)}, u32[]{:S(2)}, u32[]{:S(2)}) collective-permute-start(bf16[12,8,256]{2,1,0:T(8,128)(2,1)S(1)} %collective-permute-done.5), channel_id=1, source_target_pairs={{0,2},{2,4},{4,6},{6,8},{8,10},{10,12},{12,14},{14,16},{16,18},{18... | collective-permute-start | bytes 147464 | tf_op jit(solution)/shard_map/ppermute | solution.py:54
  145.5 6.2 %collective-permute-start.7 = (bf16[12,8,256]{2,1,0:T(8,128)(2,1)S(1)}, bf16[12,8,256]{2,1,0:T(8,128)(2,1)S(1)}, u32[]{:S(2)}, u32[]{:S(2)}) collective-permute-start(bf16[12,8,256]{2,1,0:T(8,128)(2,1)S(1)} %collective-permute-done.6), channel_id=1, source_target_pairs={{0,2},{2,4},{4,6},{6,8},{8,10},{10,12},{12,14},{14,16},{16,18},{18... | collective-permute-start | bytes 147464 | tf_op jit(solution)/shard_map/ppermute | solution.py:54
  151.7 6.2 %collective-permute-start.8 = (bf16[12,8,256]{2,1,0:T(8,128)(2,1)S(1)}, bf16[12,8,256]{2,1,0:T(8,128)(2,1)S(1)}, u32[]{:S(2)}, u32[]{:S(2)}) collective-permute-start(bf16[12,8,256]{2,1,0:T(8,128)(2,1)S(1)} %collective-permute-done.7), channel_id=1, source_target_pairs={{0,2},{2,4},{4,6},{6,8},{8,10},{10,12},{12,14},{14,16},{16,18},{18... | collective-permute-start | bytes 147464 | tf_op jit(solution)/shard_map/ppermute | solution.py:54
  157.9 6.2 %collective-permute-start.9 = (bf16[12,8,256]{2,1,0:T(8,128)(2,1)S(1)}, bf16[12,8,256]{2,1,0:T(8,128)(2,1)S(1)}, u32[]{:S(2)}, u32[]{:S(2)}) collective-permute-start(bf16[12,8,256]{2,1,0:T(8,128)(2,1)S(1)} %collective-permute-done.8), channel_id=1, source_target_pairs={{0,2},{2,4},{4,6},{6,8},{8,10},{10,12},{12,14},{14,16},{16,18},{18... | collective-permute-start | bytes 147464 | tf_op jit(solution)/shard_map/ppermute | solution.py:54
  164.1 6.2 %collective-permute-start.10 = (bf16[12,8,256]{2,1,0:T(8,128)(2,1)S(1)}, bf16[12,8,256]{2,1,0:T(8,128)(2,1)S(1)}, u32[]{:S(2)}, u32[]{:S(2)}) collective-permute-start(bf16[12,8,256]{2,1,0:T(8,128)(2,1)S(1)} %collective-permute-done.9), channel_id=1, source_target_pairs={{0,2},{2,4},{4,6},{6,8},{8,10},{10,12},{12,14},{14,16},{16,18},{18... | collective-permute-start | bytes 147464 | tf_op jit(solution)/shard_map/ppermute | solution.py:54
  170.3 6.2 %collective-permute-start.11 = (bf16[12,8,256]{2,1,0:T(8,128)(2,1)S(1)}, bf16[12,8,256]{2,1,0:T(8,128)(2,1)S(1)}, u32[]{:S(2)}, u32[]{:S(2)}) collective-permute-start(bf16[12,8,256]{2,1,0:T(8,128)(2,1)S(1)} %collective-permute-done.10), channel_id=1, source_target_pairs={{0,2},{2,4},{4,6},{6,8},{8,10},{10,12},{12,14},{14,16},{16,18},{18... | collective-permute-start | bytes 147464 | tf_op jit(solution)/shard_map/ppermute | solution.py:54
  176.6 6.2 %collective-permute-start.12 = (bf16[12,8,256]{2,1,0:T(8,128)(2,1)S(1)}, bf16[12,8,256]{2,1,0:T(8,128)(2,1)S(1)}, u32[]{:S(2)}, u32[]{:S(2)}) collective-permute-start(bf16[12,8,256]{2,1,0:T(8,128)(2,1)S(1)} %collective-permute-done.11), channel_id=1, source_target_pairs={{0,2},{2,4},{4,6},{6,8},{8,10},{10,12},{12,14},{14,16},{16,18},{18... | collective-permute-start | bytes 147464 | tf_op jit(solution)/shard_map/ppermute | solution.py:54
  182.8 6.2 %collective-permute-start.13 = (bf16[12,8,256]{2,1,0:T(8,128)(2,1)S(1)}, bf16[12,8,256]{2,1,0:T(8,128)(2,1)S(1)}, u32[]{:S(2)}, u32[]{:S(2)}) collective-permute-start(bf16[12,8,256]{2,1,0:T(8,128)(2,1)S(1)} %collective-permute-done.12), channel_id=1, source_target_pairs={{0,2},{2,4},{4,6},{6,8},{8,10},{10,12},{12,14},{14,16},{16,18},{18... | collective-permute-start | bytes 147464 | tf_op jit(solution)/shard_map/ppermute | solution.py:54
  189.0 6.2 %collective-permute-start.14 = (bf16[12,8,256]{2,1,0:T(8,128)(2,1)S(1)}, bf16[12,8,256]{2,1,0:T(8,128)(2,1)S(1)}, u32[]{:S(2)}, u32[]{:S(2)}) collective-permute-start(bf16[12,8,256]{2,1,0:T(8,128)(2,1)S(1)} %collective-permute-done.13), channel_id=1, source_target_pairs={{0,2},{2,4},{4,6},{6,8},{8,10},{10,12},{12,14},{14,16},{16,18},{18... | collective-permute-start | bytes 147464 | tf_op jit(solution)/shard_map/ppermute | solution.py:54
  216.0 2.6 %copy-start.2 = (bf16[768,768]{1,0:T(8,128)(2,1)S(1)}, bf16[768,768]{1,0:T(8,128)(2,1)}, u32[]{:S(2)}) copy-start(bf16[768,768]{1,0:T(8,128)(2,1)} %param.11) | copy-start | bytes 3538948
Sparse Core Ops, SparseCore 0:
  12.1 25.4 all-gather.4
  41.2 59.5 reduce-scatter.1
  192.1 23.8 all-gather.2
